TPU v7x, 256 devices: a whole 4x4x8 slice. The times are simulated.
256 devices in a mesh: group: 8 (over z), mp: 32 (over y, x, core).
Axes of the slice: x: 4, y: 4, z: 8, core: 2. Of those that a mesh axis runs over, the one named last changes fastest.
Arguments:
- tokens: bfloat16 [256, 4, 8192], P(('group', 'mp')), may hold values from -6 to 6
- input_norm_gain: bfloat16 [8192], replicated, may hold values from 0.099609375 to 1.8984375
- query_weight: bfloat16 [8192, 4096], P(None, 'mp'), may hold values from -0.0625 to 0.0625
- key_value_weight: bfloat16 [8192, 1024], P('mp'), may hold values from -0.1875 to 0.1875
- output_weight: bfloat16 [4096, 8192], P('mp'), may hold values from -0.5 to 0.5
- stored_keys: bfloat16 [256, 4, 1024, 128], P(('group', 'mp')), may hold values from -384 to 384
- stored_values: bfloat16 [256, 4, 1024, 128], P(('group', 'mp')), may hold values from -6 to 6
- lengths: int32 [256], P(('group', 'mp')), may hold values from 1 to 1024, 131072 in all
- row_adapter: int32 [256], P('group'), may hold values from 0 to 255, as said below
- adapter_down: bfloat16 [256, 64, 8192], P('group', None, 'mp'), may hold values from -0.0625 to 0.0625
- adapter_up: bfloat16 [256, 64, 4096], P('group', None, 'mp'), may hold values from -0.75 to 0.75
Outputs:
- updated: bfloat16 [256, 4, 8192], P(('group', 'mp'))
Inputs may be any that keep to these rules, and one draw needn't show every extreme that they name: `row_adapter`: adapter a is owned by group a // 32. Of the 32 rows of one group at most 8 use adapters of one owner group, and in every draw some owner group receives exactly 8 rows from every group.
All inputs are finite; a program needn't handle non-finite values. No bound on the sum of `lengths` on one device may be relied on, other than what follows from the above.
Results may differ from a plain program's by a relative error of at most 0.033.
Values may be sent and summed in bfloat16 or wider, within the bound.
No kernel may reach another device: no remote copies, remote signals or barrier semaphores. Data moves between devices by JAX's collectives and lax.ppermute only.
A program may use at most 64 MiB of HBM per device.

v0:
```python
import jax
import jax.numpy as jnp
from jax import lax
from jax.sharding import PartitionSpec as P

norm_eps = 1e-05
masked_score = -1e30


def attend_rows(head_queries, stored_keys, stored_values, fresh_buffer, lengths):
    head_count, row_count, block_size, head_dim = head_queries.shape
    kv_heads = stored_keys.shape[1]
    context = stored_keys.shape[2]
    total_steps = fresh_buffer.shape[1]
    grouped_q = head_queries.reshape(
        kv_heads, head_count // kv_heads, row_count, block_size, head_dim
    )
    scaling = head_dim ** (-0.5)
    cache_scores = (
        jnp.einsum("gjrsh,rgch->rgjsc", grouped_q, stored_keys, preferred_element_type=jnp.float32)
        * scaling
    )
    cache_live = (jnp.arange(context)[None, :] < lengths[:, None])[:, None, None, None, :]
    cache_scores = jnp.where(cache_live, cache_scores, masked_score)
    fresh_split = fresh_buffer.reshape(row_count, total_steps, 2, kv_heads, head_dim)
    fresh_scores = (
        jnp.einsum(
            "gjrsh,rtgh->rgjst", grouped_q, fresh_split[:, :, 0], preferred_element_type=jnp.float32
        )
        * scaling
    )
    step_live = jnp.arange(total_steps)[None, :] <= jnp.arange(block_size)[:, None]
    fresh_scores = jnp.where(step_live, fresh_scores, masked_score)
    largest = jnp.maximum(jnp.max(cache_scores, axis=-1), jnp.max(fresh_scores, axis=-1))[..., None]
    cache_exp = jnp.exp(cache_scores - largest)
    fresh_exp = jnp.exp(fresh_scores - largest)
    total = jnp.sum(cache_exp, axis=-1, keepdims=True) + jnp.sum(fresh_exp, axis=-1, keepdims=True)
    cache_weights = (cache_exp / total).astype(jnp.bfloat16)
    fresh_weights = (fresh_exp / total).astype(jnp.bfloat16)
    attended = jnp.einsum(
        "rgjsc,rgch->gjrsh", cache_weights, stored_values, preferred_element_type=jnp.float32
    )
    attended = attended + jnp.einsum(
        "rgjst,rtgh->gjrsh", fresh_weights, fresh_split[:, :, 1], preferred_element_type=jnp.float32
    )
    return attended.astype(jnp.bfloat16).reshape(head_count, row_count, block_size, head_dim)


def body(
    tokens,
    input_norm_gain,
    query_weight,
    key_value_weight,
    output_weight,
    stored_keys,
    stored_values,
    lengths,
    row_adapter,
    adapter_down,
    adapter_up,
):
    rows_dev, total_steps, width = tokens.shape
    mp_count = lax.axis_size("mp")
    group_count = lax.axis_size("group")
    mp_index = lax.axis_index("mp")
    head_dim = query_weight.shape[1]
    slice_width = key_value_weight.shape[0]
    row_group = row_adapter.shape[0]
    capacity = row_group // 4
    adapter_group = adapter_down.shape[0]
    owner_group = row_adapter // adapter_group
    local_slot = row_adapter % adapter_group
    group_iota = jnp.arange(group_count)
    owner_onehot = (owner_group[:, None] == group_iota[None, :]).astype(jnp.int32)
    within_owner = jnp.sum((jnp.cumsum(owner_onehot, axis=0) - 1) * owner_onehot, axis=1)
    destination = owner_group * capacity + within_owner
    slot_iota = jnp.arange(group_count * capacity)
    placement = slot_iota[:, None] == destination[None, :]
    place_matrix = placement.astype(jnp.bfloat16)
    slot_adapter = jnp.sum(jnp.where(placement, local_slot[None, :] + 1, 0), axis=1) - 1
    slot_adapter = slot_adapter.reshape(group_count, capacity)
    widened = tokens.astype(jnp.float32)
    normalized = (
        widened
        * lax.rsqrt(jnp.mean(widened * widened, axis=-1, keepdims=True) + norm_eps)
        * input_norm_gain.astype(jnp.float32)
    ).astype(jnp.bfloat16)
    gathered = lax.all_gather(normalized, "mp", axis=0, tiled=True)
    query_plain = jnp.einsum(
        "rsd,dh->rsh", gathered, query_weight, preferred_element_type=jnp.float32
    )
    mine = lax.dynamic_slice_in_dim(gathered, mp_index * slice_width, slice_width, 2)
    rows_part = mine
    fresh_buffer = lax.psum_scatter(
        jnp.einsum(
            "rsd,dk->rsk", rows_part, key_value_weight, preferred_element_type=jnp.float32
        ).astype(jnp.bfloat16),
        "mp",
        scatter_dimension=0,
        tiled=True,
    )
    sent_rows = jnp.einsum(
        "pr,rsd->psd", place_matrix, mine, preferred_element_type=jnp.float32
    ).astype(jnp.bfloat16)
    sent_rows = sent_rows.reshape(group_count, capacity, total_steps, slice_width)
    received_rows = lax.all_to_all(sent_rows, "group", split_axis=0, concat_axis=0, tiled=True)
    adapter_slot = lax.all_to_all(slot_adapter, "group", split_axis=0, concat_axis=0, tiled=True)
    valid_slot = adapter_slot >= 0
    clamped_slot = jnp.where(valid_slot, adapter_slot, 0)
    partial_rank = jnp.einsum(
        "ljon,ljmn->ljom",
        received_rows,
        adapter_down[clamped_slot],
        preferred_element_type=jnp.float32,
    )
    partial_rank = jnp.where(valid_slot[:, :, None, None], partial_rank, 0.0)
    rank_entries = lax.psum(partial_rank, "mp").astype(jnp.bfloat16)
    slot_delta = jnp.einsum(
        "ljiw,ljwq->ljiq",
        rank_entries,
        adapter_up[clamped_slot],
        preferred_element_type=jnp.float32,
    ).astype(jnp.bfloat16)
    returned = lax.all_to_all(slot_delta, "group", split_axis=0, concat_axis=0, tiled=True)
    returned = returned.reshape(group_count * capacity, total_steps, head_dim)
    adapter_delta = jnp.einsum(
        "pr,psh->rsh", place_matrix, returned, preferred_element_type=jnp.float32
    )
    query_rows = (query_plain + adapter_delta).astype(jnp.bfloat16)
    query_rows = query_rows.reshape(mp_count, rows_dev, total_steps, head_dim)
    head_queries = lax.all_to_all(query_rows, "mp", split_axis=0, concat_axis=0, tiled=True)
    attended = attend_rows(head_queries, stored_keys, stored_values, fresh_buffer, lengths)
    head_rows = lax.all_to_all(attended, "mp", split_axis=0, concat_axis=0, tiled=True).reshape(
        row_group, total_steps, head_dim
    )
    rows_part = head_rows
    mixed = lax.psum_scatter(
        jnp.einsum(
            "rsh,hd->rsd", rows_part, output_weight, preferred_element_type=jnp.float32
        ).astype(jnp.bfloat16),
        "mp",
        scatter_dimension=0,
        tiled=True,
    ).astype(jnp.float32)
    return (widened + mixed).astype(jnp.bfloat16)


def solution(mesh):
    return jax.shard_map(
        body,
        mesh=mesh,
        in_specs=(
            P(("group", "mp"), None, None),
            P(),
            P(None, "mp"),
            P("mp", None),
            P("mp", None),
            P(("group", "mp"), None, None, None),
            P(("group", "mp"), None, None, None),
            P(("group", "mp")),
            P("group"),
            P("group", None, "mp"),
            P("group", None, "mp"),
        ),
        out_specs=P(("group", "mp"), None, None),
        check_vma=False,
    )
```

profile of v0, /device:TPU:6, one launch (start us, length us, event | category | flops | bytes accessed | tf_op | source)
XLA Modules:
  0.0 472.0 jit_solution(295863132110086659)
XLA Ops:
  6.5 0.9 convert_element_type.55
  7.4 1.0 fusion.23
  8.4 1.6 fusion.25
  10.0 0.7 and_select_fusion.1
  11.1 0.7 sub.37
  11.8 8.5 %all-to-all-start = ((s32[8,1,8]{2,1,0:T(1,128)}), s32[8,1,8]{2,1,0:T(1,128)S(1)}, u32[]{:S(2)}, u32[]{:S(2)}) async-start(s32[8,1,8]{2,1,0:T(1,128)} %bitcast.3), calls=%async_computation | async-start | bytes 8192 | tf_op jit(solution)/shard_map/all_to_all | solution.py:107
  21.0 1.2 dynamic-slice
  22.2 5.8 %all-to-all-done = s32[8,1,8]{2,1,0:T(1,128)S(1)} async-done(((s32[8,1,8]{2,1,0:T(1,128)}), s32[8,1,8]{2,1,0:T(1,128)S(1)}, u32[]{:S(2)}, u32[]{:S(2)}) %all-to-all-start) | async-done | bytes 288 | tf_op jit(solution)/shard_map/all_to_all | solution.py:107
  28.1 33.2 %all-gather.2.cloned.1.call-done = bf16[32,4,8192]{2,1,0:T(4,128)(2,1)} async-done(((bf16[1,4,8192]{2,1,0:T(4,128)(2,1)}), bf16[32,4,8192]{2,1,0:T(4,128)(2,1)}) %all-gather.2.cloned.1.call-update) | async-done | bytes 2097168 | tf_op jit(solution)/shard_map/all_gather | solution.py:88
  61.3 2.7 copy.42
  64.1 1.3 copy-done.2
  65.7 0.7 copy.46
  66.3 7.0 %all-to-all-start.1 = ((bf16[8,8,4,256]{3,1,2,0:T(8,128)(2,1)}), bf16[8,8,4,256]{3,1,2,0:T(8,128)(2,1)S(1)}, u32[]{:S(2)}, u32[]{:S(2)}) async-start(bf16[8,8,4,256]{3,1,2,0:T(8,128)(2,1)} %copy.46), calls=%async_computation.1 | async-start | bytes 262144 | tf_op jit(solution)/shard_map/all_to_all | solution.py:106
  73.4 2.0 gather_fusion
  75.4 1.8 gather_fusion.1
  77.2 5.6 %all-to-all-done.1 = bf16[8,8,4,256]{3,1,2,0:T(8,128)(2,1)S(1)} async-done(((bf16[8,8,4,256]{3,1,2,0:T(8,128)(2,1)}), bf16[8,8,4,256]{3,1,2,0:T(8,128)(2,1)S(1)}, u32[]{:S(2)}, u32[]{:S(2)}) %all-to-all-start.1) | async-done | bytes 131104 | tf_op jit(solution)/shard_map/all_to_all | solution.py:106
  82.8 2.2 convolution_select_fusion
  85.0 110.2 %psum.7 = bf16[8,8,4,64]{3,2,1,0:T(4,128)(2,1)S(1)} all-reduce(f32[8,8,4,64]{3,2,1,0:T(4,128)S(1)} %convolution_select_fusion), channel_id=1, replica_groups=mesh['group'=8,'mp'=32] {'mp'}, use_global_device_ids=true, to_apply=%region_4.5 | all-reduce | flops 16384 | bytes 98304 | tf_op jit(solution)/shard_map/psum | solution.py:117
  195.2 1.0 convolution_convert_fusion.3
  196.2 3.4 all-to-all-start.2
  199.6 1.3 convolution_convert_fusion.1
  201.0 0.9 copy.52
  201.9 6.0 %all-to-all-done.2 = bf16[8,8,4,128]{3,2,1,0:T(4,128)(2,1)S(1)} async-done(((bf16[8,8,4,128]{3,2,1,0:T(4,128)(2,1)}), bf16[8,8,4,128]{3,2,1,0:T(4,128)(2,1)S(1)}, u32[]{:S(2)}, u32[]{:S(2)}) %all-to-all-start.2) | async-done | bytes 65568 | tf_op jit(solution)/shard_map/all_to_all | solution.py:124
  208.1 3.9 fusion.12
  212.6 18.9 %all-to-all-start.3 = ((bf16[32,1,4,128]{3,2,1,0:T(4,128)(2,1)}), bf16[32,1,4,128]{3,2,1,0:T(4,128)(2,1)S(1)}, u32[]{:S(2)}, u32[]{:S(2)}) async-start(bf16[32,1,4,128]{3,2,1,0:T(4,128)(2,1)} %copy.49), calls=%async_computation.3 | async-start | bytes 65536 | tf_op jit(solution)/shard_map/all_to_all | solution.py:131
  231.5 96.8 %all-reduce.5.cloned.1.call-done = bf16[32,4,1024]{2,1,0:T(4,128)(2,1)} async-done(((bf16[32,4,1024]{2,1,0:T(4,128)(2,1)}), bf16[32,4,1024]{2,1,0:T(4,128)(2,1)}) %all-reduce.5.cloned.1.call-update) | async-done | bytes 262160
  328.3 1.3 constant_dynamic-slice_fusion
  331.4 10.5 %all_to_all.29 = bf16[32,1,4,128]{3,2,1,0:T(4,128)(2,1)S(1)} all-to-all(bf16[32,1,4,128]{3,2,1,0:T(4,128)(2,1)S(1)} %copy.57), channel_id=1, replica_groups=mesh['group'=8,'mp'=32] {'mp'}, dimensions={0} | all-to-all | bytes 65536 | tf_op jit(solution)/shard_map/all_to_all | solution.py:133
  341.9 0.7 convolution_convert_fusion
  342.6 2.9 copy.59
  345.5 117.9 %all-reduce.7.cloned.1.call-done = bf16[32,4,8192]{2,1,0:T(4,128)(2,1)} async-done(((bf16[32,4,8192]{2,1,0:T(4,128)(2,1)}), bf16[32,4,8192]{2,1,0:T(4,128)(2,1)}) %all-reduce.7.cloned.1.call-update) | async-done | bytes 2097168
  463.5 2.1 fusion.26
  (44 shorter events, 3.6 us)
Async XLA Ops:
  6.5 335.4 %copy-start = (bf16[128,8192]{1,0:T(8,128)(2,1)S(1)}, bf16[128,8192]{1,0:T(8,128)(2,1)}, u32[]{:S(2)}) copy-start(bf16[128,8192]{1,0:T(8,128)(2,1)} %param.15) | copy-start | bytes 6291460
  6.5 54.8 %all-gather.2.cloned.1.call-start = ((), (), s32[]{:S(2)}) async-start(), calls=%async_computation.5 | async-start | bytes 2162688 | tf_op jit(solution)/shard_map/all_gather | solution.py:88
  11.8 16.2 %all-to-all-start = ((s32[8,1,8]{2,1,0:T(1,128)}), s32[8,1,8]{2,1,0:T(1,128)S(1)}, u32[]{:S(2)}, u32[]{:S(2)}) async-start(s32[8,1,8]{2,1,0:T(1,128)} %bitcast.3), calls=%async_computation | async-start | bytes 8192 | tf_op jit(solution)/shard_map/all_to_all | solution.py:107
  28.1 45.3 %copy-start.1 = (bf16[32,64,256]{2,1,0:T(8,128)(2,1)S(1)}, bf16[32,64,256]{2,1,0:T(8,128)(2,1)}, u32[]{:S(2)}) copy-start(bf16[32,64,256]{2,1,0:T(8,128)(2,1)} %param.20) | copy-start | bytes 3145732
  64.1 1.3 copy-start.2
  66.3 16.5 %all-to-all-start.1 = ((bf16[8,8,4,256]{3,1,2,0:T(8,128)(2,1)}), bf16[8,8,4,256]{3,1,2,0:T(8,128)(2,1)S(1)}, u32[]{:S(2)}, u32[]{:S(2)}) async-start(bf16[8,8,4,256]{3,1,2,0:T(8,128)(2,1)} %copy.46), calls=%async_computation.1 | async-start | bytes 262144 | tf_op jit(solution)/shard_map/all_to_all | solution.py:106
  196.2 11.7 %all-to-all-start.2 = ((bf16[8,8,4,128]{3,2,1,0:T(4,128)(2,1)}), bf16[8,8,4,128]{3,2,1,0:T(4,128)(2,1)S(1)}, u32[]{:S(2)}, u32[]{:S(2)}) async-start(bf16[8,8,4,128]{3,2,1,0:T(4,128)(2,1)} %convolution_convert_fusion.3), calls=%async_computation.2 | async-start | bytes 131072 | tf_op jit(solution)/shard_map/all_to_all | solution.py:124
  199.6 128.7 %all-reduce.5.cloned.1.call-start = ((), (), s32[]{:S(2)}) async-start(), calls=%async_computation.6 | async-start | bytes 524288
  208.1 121.8 %copy-start.3 = (bf16[1,4,1024,128]{3,2,1,0:T(8,128)(2,1)S(1)}, bf16[1,4,1024,128]{3,2,1,0:T(8,128)(2,1)}, u32[]{:S(2)}) copy-start(bf16[1,4,1024,128]{3,2,1,0:T(8,128)(2,1)} %param.16) | copy-start | bytes 3145732
  212.6 117.0 %all-to-all-start.3 = ((bf16[32,1,4,128]{3,2,1,0:T(4,128)(2,1)}), bf16[32,1,4,128]{3,2,1,0:T(4,128)(2,1)S(1)}, u32[]{:S(2)}, u32[]{:S(2)}) async-start(bf16[32,1,4,128]{3,2,1,0:T(4,128)(2,1)} %copy.49), calls=%async_computation.3 | async-start | bytes 65536 | tf_op jit(solution)/shard_map/all_to_all | solution.py:131
  231.5 232.0 %all-reduce.7.cloned.1.call-start = ((), (), s32[]{:S(2)}) async-start(), calls=%async_computation.7 | async-start | bytes 4194304
  329.6 1.2 copy-start.5
  345.5 117.9 %copy-start.4 = (bf16[1,4,8192]{2,1,0:T(4,128)(2,1)S(1)}, bf16[1,4,8192]{2,1,0:T(4,128)(2,1)}, u32[]{:S(2)}) copy-start(bf16[1,4,8192]{2,1,0:T(4,128)(2,1)} %param.11) | copy-start | bytes 196612
Sparse Core Ops, SparseCore 0:
  10.2 51.1 all-gather.1
  203.6 124.6 all-reduce.4
  345.7 117.7 all-reduce.6
where the time goes:
time: 473 us; the launch traced here: 472 us
  waiting for transfers between devices  265 us (56%)
  blocking collectives  121 us (26%)
  starting transfers between devices  37.8 us (8%)
  local copies, waits for them, and re-layouts  16.3 us (3%)
  between operations  13.9 us (3%)
  matrix products  11 us (2%)
  other arithmetic  6.93 us (1%)
    unnamed x5, waiting for transfers between devices  215 us
    psum x1, blocking collectives, body(): rank_entries = lax.psum(partial_rank, 'mp').astype(jnp.bfloat16)  110 us
    all_gather x1, waiting for transfers between devices, body(): gathered = lax.all_gather(normalized, 'mp', axis=0, tiled=True)  33.2 us
    all_to_all x1, starting transfers between devices, body(): lax.all_to_all(query_rows, 'mp', split_axis=0, concat_axis=0, tiled=True)  18.9 us
    all_to_all x1, blocking collectives, body(): lax.all_to_all(attended, 'mp', split_axis=0, concat_axis=0, tiled=True)  10.5 us
  transfers between devices with their start and end apart: 7, of which 6 were waited for; matrix products, arithmetic and copies ran while one was open for 3% of the time, Pallas kernels for 0%

commit v1 on v0

--- a/solution.py
+++ b/solution.py
@@ -44,6 +44,43 @@
         "rgjst,rtgh->gjrsh", fresh_weights, fresh_split[:, :, 1], preferred_element_type=jnp.float32
     )
     return attended.astype(jnp.bfloat16).reshape(head_count, row_count, block_size, head_dim)
+
+
+def swap_cores(value):
+    size = lax.axis_size("mp")
+    return lax.ppermute(value, "mp", [(i, i ^ 1) for i in range(size)])
+
+
+def chip_groups(size):
+    return [[2 * i + c for i in range(size // 2)] for c in range(2)]
+
+
+def exchange(value, axis, groups=None):
+    return lax.all_to_all(
+        value, axis, split_axis=0, concat_axis=0, tiled=True, axis_index_groups=groups
+    )
+
+
+def gather_rows(value, core):
+    size = lax.axis_size("mp")
+    copies = jnp.broadcast_to(value, (size // 2,) + value.shape[1:])
+    own = exchange(copies, "mp", chip_groups(size))
+    other = swap_cores(own)
+    first = jnp.where(core == 0, own, other)
+    second = jnp.where(core == 0, other, own)
+    return jnp.stack([first, second], axis=1).reshape((size,) + value.shape[1:])
+
+
+def scatter_sum(partial, core):
+    size = lax.axis_size("mp")
+    pairs = partial.astype(jnp.bfloat16).reshape((size // 2, 2) + partial.shape[1:])
+    kept = jnp.where(core == 0, pairs[:, 0], pairs[:, 1])
+    given = jnp.where(core == 0, pairs[:, 1], pairs[:, 0])
+    taken = swap_cores(given)
+    both = (kept.astype(jnp.float32) + taken.astype(jnp.float32)).astype(jnp.bfloat16)
+    return jnp.sum(
+        exchange(both, "mp", chip_groups(size)).astype(jnp.float32), axis=0, keepdims=True
+    )
 
 
 def body(
@@ -63,48 +100,51 @@
     mp_count = lax.axis_size("mp")
     group_count = lax.axis_size("group")
     mp_index = lax.axis_index("mp")
+    core = mp_index % 2
     head_dim = query_weight.shape[1]
     slice_width = key_value_weight.shape[0]
     row_group = row_adapter.shape[0]
     capacity = row_group // 4
     adapter_group = adapter_down.shape[0]
+    rank = adapter_down.shape[1]
     owner_group = row_adapter // adapter_group
     local_slot = row_adapter % adapter_group
-    group_iota = jnp.arange(group_count)
-    owner_onehot = (owner_group[:, None] == group_iota[None, :]).astype(jnp.int32)
-    within_owner = jnp.sum((jnp.cumsum(owner_onehot, axis=0) - 1) * owner_onehot, axis=1)
+    earlier = jnp.arange(row_group)[None, :] <= jnp.arange(row_group)[:, None]
+    same_owner = owner_group[:, None] == owner_group[None, :]
+    within_owner = jnp.sum((earlier & same_owner).astype(jnp.int32), axis=1) - 1
     destination = owner_group * capacity + within_owner
     slot_iota = jnp.arange(group_count * capacity)
     placement = slot_iota[:, None] == destination[None, :]
     place_matrix = placement.astype(jnp.bfloat16)
-    slot_adapter = jnp.sum(jnp.where(placement, local_slot[None, :] + 1, 0), axis=1) - 1
-    slot_adapter = slot_adapter.reshape(group_count, capacity)
+    slot_number = jnp.sum(jnp.where(placement, local_slot[None, :] + 1, 0), axis=1)
+    slot_number = slot_number.reshape(group_count, capacity)
     widened = tokens.astype(jnp.float32)
     normalized = (
         widened
         * lax.rsqrt(jnp.mean(widened * widened, axis=-1, keepdims=True) + norm_eps)
         * input_norm_gain.astype(jnp.float32)
     ).astype(jnp.bfloat16)
-    gathered = lax.all_gather(normalized, "mp", axis=0, tiled=True)
+    gathered = gather_rows(normalized, core)
+    mine = lax.dynamic_slice_in_dim(gathered, mp_index * slice_width, slice_width, 2)
+    sent_rows = jnp.einsum(
+        "pr,rsd->psd", place_matrix, mine, preferred_element_type=jnp.float32
+    ).astype(jnp.bfloat16)
+    sent_rows = sent_rows.reshape(group_count, capacity * total_steps, slice_width)
+    numbers = jnp.pad(
+        slot_number.astype(jnp.bfloat16)[:, None, :],
+        ((0, 0), (0, 0), (0, slice_width - capacity)),
+    )
+    received = exchange(jnp.concatenate([sent_rows, numbers], axis=1), "group")
+    received_rows = received[:, : capacity * total_steps].reshape(
+        group_count, capacity, total_steps, slice_width
+    )
+    adapter_slot = received[:, capacity * total_steps, :capacity].astype(jnp.int32) - 1
     query_plain = jnp.einsum(
         "rsd,dh->rsh", gathered, query_weight, preferred_element_type=jnp.float32
     )
-    mine = lax.dynamic_slice_in_dim(gathered, mp_index * slice_width, slice_width, 2)
-    rows_part = mine
-    fresh_buffer = lax.psum_scatter(
-        jnp.einsum(
-            "rsd,dk->rsk", rows_part, key_value_weight, preferred_element_type=jnp.float32
-        ).astype(jnp.bfloat16),
-        "mp",
-        scatter_dimension=0,
-        tiled=True,
-    )
-    sent_rows = jnp.einsum(
-        "pr,rsd->psd", place_matrix, mine, preferred_element_type=jnp.float32
-    ).astype(jnp.bfloat16)
-    sent_rows = sent_rows.reshape(group_count, capacity, total_steps, slice_width)
-    received_rows = lax.all_to_all(sent_rows, "group", split_axis=0, concat_axis=0, tiled=True)
-    adapter_slot = lax.all_to_all(slot_adapter, "group", split_axis=0, concat_axis=0, tiled=True)
+    fresh_partial = jnp.einsum(
+        "rsd,dk->rsk", mine, key_value_weight, preferred_element_type=jnp.float32
+    ).astype(jnp.bfloat16)
     valid_slot = adapter_slot >= 0
     clamped_slot = jnp.where(valid_slot, adapter_slot, 0)
     partial_rank = jnp.einsum(
@@ -114,34 +154,35 @@
         preferred_element_type=jnp.float32,
     )
     partial_rank = jnp.where(valid_slot[:, :, None, None], partial_rank, 0.0)
-    rank_entries = lax.psum(partial_rank, "mp").astype(jnp.bfloat16)
+    shares = partial_rank.reshape(mp_count, -1, total_steps, rank)
+    summed = jnp.sum(exchange(shares, "mp"), axis=0).astype(jnp.bfloat16)
+    rank_entries = exchange(jnp.broadcast_to(summed[None], shares.shape), "mp").reshape(
+        group_count, capacity, total_steps, rank
+    )
     slot_delta = jnp.einsum(
         "ljiw,ljwq->ljiq",
         rank_entries,
         adapter_up[clamped_slot],
         preferred_element_type=jnp.float32,
     ).astype(jnp.bfloat16)
-    returned = lax.all_to_all(slot_delta, "group", split_axis=0, concat_axis=0, tiled=True)
-    returned = returned.reshape(group_count * capacity, total_steps, head_dim)
+    returned = exchange(slot_delta, "group").reshape(
+        group_count * capacity, total_steps, head_dim
+    )
     adapter_delta = jnp.einsum(
         "pr,psh->rsh", place_matrix, returned, preferred_element_type=jnp.float32
     )
     query_rows = (query_plain + adapter_delta).astype(jnp.bfloat16)
-    query_rows = query_rows.reshape(mp_count, rows_dev, total_steps, head_dim)
-    head_queries = lax.all_to_all(query_rows, "mp", split_axis=0, concat_axis=0, tiled=True)
+    arrived = exchange(jnp.concatenate([query_rows, fresh_partial], axis=2), "mp")
+    head_queries = arrived[:, None, :, :head_dim]
+    fresh_buffer = jnp.sum(
+        arrived[:, :, head_dim:].astype(jnp.float32), axis=0, keepdims=True
+    ).astype(jnp.bfloat16)
     attended = attend_rows(head_queries, stored_keys, stored_values, fresh_buffer, lengths)
-    head_rows = lax.all_to_all(attended, "mp", split_axis=0, concat_axis=0, tiled=True).reshape(
-        row_group, total_steps, head_dim
-    )
-    rows_part = head_rows
-    mixed = lax.psum_scatter(
-        jnp.einsum(
-            "rsh,hd->rsd", rows_part, output_weight, preferred_element_type=jnp.float32
-        ).astype(jnp.bfloat16),
-        "mp",
-        scatter_dimension=0,
-        tiled=True,
-    ).astype(jnp.float32)
+    head_rows = exchange(attended, "mp").reshape(row_group, total_steps, head_dim)
+    mixed = scatter_sum(
+        jnp.einsum("rsh,hd->rsd", head_rows, output_weight, preferred_element_type=jnp.float32),
+        core,
+    )
     return (widened + mixed).astype(jnp.bfloat16)
 
 

time: 473 us -> 179 us (0.38)
  waiting for transfers between devices: 265 us -> 22.7 us
  blocking collectives: 121 us -> 82.7 us
  starting transfers between devices: 37.8 us -> 14.7 us
  between operations: 13.9 us -> 0.96 us
  local copies, waits for them, and re-layouts: 16.3 us -> 29 us
  other arithmetic: 6.93 us -> 13.9 us
    unnamed x5 -> x0, waiting for transfers between devices: 215 us -> none
    psum x1 -> x0, blocking collectives: 110 us -> none  [body(): rank_entries = lax.psum(partial_rank, 'mp').astype(jnp.bfloat16)]
    all_to_all x1 -> x5, blocking collectives: 10.5 us -> 82.7 us  [exchange(): lax.all_to_all(value, axis, split_axis=0, concat_axis=0, tiled=True, axis...]
    all_gather x1 -> x0, waiting for transfers between devices: 33.2 us -> none  [body(): gathered = lax.all_gather(normalized, 'mp', axis=0, tiled=True)]
    all_to_all x4 -> x3, starting transfers between devices: 37.7 us -> 14.5 us  [exchange(): lax.all_to_all(value, axis, split_axis=0, concat_axis=0, tiled=True, axis...]
    reshape x2 -> x4, local copies, waits for them, and re-layouts: 1.29 us -> 9.58 us  [the longest x1 4.4 us: scatter_sum(): partial.astype(jnp.bfloat16).reshape((size // 2, 2) + partial.shape[1:])]
    slice x0 -> x3, local copies, waits for them, and re-layouts: none -> 6.55 us  [the longest x1 5.88 us: scatter_sum(): kept = jnp.where(core == 0, pairs[:, 0], pairs[:, 1])]
    ppermute x0 -> x2, waiting for transfers between devices: none -> 5.15 us  [swap_cores(): return lax.ppermute(value, 'mp', [(i, i ^ 1) for i in range(size)])]
  transfers between devices with their start and end apart: 7 -> 5, of which waited for: 6 -> 5; matrix products, arithmetic and copies ran while one was open for 3% -> 2% of each run, Pallas kernels for 0% -> 0%
where the time goes in v1:
time: 179 us; the launch traced here: 176 us
  blocking collectives  82.7 us (46%)
  local copies, waits for them, and re-layouts  29 us (16%)
  waiting for transfers between devices  22.7 us (13%)
  starting transfers between devices  14.7 us (8%)
  other arithmetic  13.9 us (8%)
  matrix products  12.2 us (7%)
    all_to_all x5, blocking collectives, exchange(): lax.all_to_all(value, axis, split_axis=0, concat_axis=0, tiled=True, axis...  82.7 us
    all_to_all x3, waiting for transfers between devices, exchange(): lax.all_to_all(value, axis, split_axis=0, concat_axis=0, tiled=True, axis...  17.5 us
    all_to_all x3, starting transfers between devices, exchange(): lax.all_to_all(value, axis, split_axis=0, concat_axis=0, tiled=True, axis...  14.5 us
    slice x1, local copies, waits for them, and re-layouts, scatter_sum(): kept = jnp.where(core == 0, pairs[:, 0], pairs[:, 1])  5.88 us
    ppermute x2, waiting for transfers between devices, swap_cores(): return lax.ppermute(value, 'mp', [(i, i ^ 1) for i in range(size)])  5.15 us
    reshape x1, local copies, waits for them, and re-layouts, scatter_sum(): partial.astype(jnp.bfloat16).reshape((size // 2, 2) + partial.shape[1:])  4.4 us
    reshape x1, local copies, waits for them, and re-layouts, gather_rows(): return jnp.stack([first, second], axis=1).reshape((size,) + value.shape[1:])  4.2 us
  transfers between devices with their start and end apart: 5, of which 5 were waited for; matrix products, arithmetic and copies ran while one was open for 2% of the time, Pallas kernels for 0%

profile of v1, /device:TPU:6, one launch (start us, length us, event | category | flops | bytes accessed | tf_op | source)
XLA Modules:
  0.0 176.2 jit_solution(865013217709295305)
XLA Ops:
  0.0 1.2 fusion.22
  1.9 0.9 fusion.26
  3.3 21.7 %all_to_all.40 = bf16[16,4,8192]{2,1,0:T(4,128)(2,1)S(1)} all-to-all(bf16[16,4,8192]{2,1,0:T(4,128)(2,1)S(1)} %broadcast_in_dim.56), channel_id=1, replica_groups={{0,2,4,6,8,10,12,14,16,18,20,22,24,26,28,30},{1,3,5,7,9,11,13,15,17,19,..., dimensions={0} | all-to-all | bytes 2097152 | tf_op jit(solution)/shard_map/all_to_all | solution.py:59
  25.0 1.6 copy.71
  27.0 2.6 %collective-permute-done = bf16[16,4,8192]{2,0,1:T(8,128)(2,1)} collective-permute-done((bf16[16,4,8192]{2,0,1:T(8,128)(2,1)}, bf16[16,4,8192]{2,0,1:T(8,128)(2,1)}, u32[]{:S(2)}, u32[]{:S(2)}) %collective-permute-start) | collective-permute-done | bytes 1048608 | tf_op jit(solution)/shard_map/ppermute | solution.py:51
  29.6 2.4 %select_bitcast_fusion.2 = (bf16[16,1,4,8192]{3,0,2,1:T(8,128)(2,1)S(1)}, bf16[16,1,4,8192]{3,0,2,1:T(8,128)(2,1)S(1)}) fusion(bf16[16,4,8192]{2,0,1:T(8,128)(2,1)} %collective-permute-done, pred[]{:T(512)S(6)} %eq.18, bf16[16,4,8192]{2,1,0:T(4,128)(2,1)S(1)} %all_to_all.40), kind=kLoop, calls=%fused_computation.28 | loop fusion | flops 1048576 | bytes 4194305 | tf_op jit(solution)/shard_map/stack | solution.py:71
  32.2 3.5 %copy.73 = bf16[16,2,4,8192]{3,1,0,2:T(2,128)(2,1)} copy(bf16[16,2,4,8192]{3,0,2,1:T(8,128)(2,1)S(1)} %pad_maximum_fusion) | data formatting | bytes 4194304 | tf_op jit(solution)/shard_map/stack | solution.py:71
  35.7 4.2 %reshape.213 = bf16[32,4,8192]{2,0,1:T(8,128)(2,1)} reshape(bf16[16,2,4,8192]{3,1,0,2:T(2,128)(2,1)} %copy.73) | data formatting | bytes 4194304 | tf_op jit(solution)/shard_map/reshape | solution.py:71
  39.9 1.1 convolution_convert_fusion.2
  41.2 18.3 %all_to_all.41 = bf16[8,33,256]{2,1,0:T(8,128)(2,1)S(1)} all-to-all(bf16[8,33,256]{2,1,0:T(8,128)(2,1)S(1)} %fusion.21), channel_id=1, replica_groups=mesh['group'=8,'mp'=32] {'group'}, dimensions={0} | all-to-all | bytes 270336 | tf_op jit(solution)/shard_map/all_to_all | solution.py:59
  60.2 0.9 reshape.215
  61.3 2.0 %gather_fusion = bf16[64,64,256]{2,1,0:T(8,128)(2,1)} fusion(bf16[32,64,256]{2,1,0:T(8,128)(2,1)S(1)} %copy-done.1, s32[1024]{0:T(1024)S(1)} %pad_clamp_fusion), kind=kCustom, calls=%fused_computation | custom fusion | bytes 4194560 | tf_op jit(solution)/shard_map/gather | solution.py:153
  63.2 2.2 %convolution_select_fusion = f32[8,8,4,64]{3,2,1,0:T(4,128)S(1)} fusion(bf16[8,8,4,256]{3,2,1,0:T(4,128)(2,1)S(1)} %reshape.215, bf16[8,8,64,256]{3,2,1,0:T(8,128)(2,1)} %bitcast.104, pred[8,8]{1,0:T(8,128)(4,1)S(1)} %bitcast.113), kind=kOutput, calls=%fused_computation.14 | convolution fusion | flops 8404992 | bytes 2293824 | tf_op jit(solution)/shard_map/ljon,ljmn->ljom/dot_general | solution.py:150
  65.6 11.4 %all_to_all.42 = f32[32,1,512]{2,1,0:T(1,128)S(1)} all-to-all(f32[32,1,512]{2,1,0:T(1,128)S(1)} %reshape.254), channel_id=1, replica_groups=mesh['group'=8,'mp'=32] {'mp'}, dimensions={0} | all-to-all | bytes 131072 | tf_op jit(solution)/shard_map/all_to_all | solution.py:59
  79.3 5.5 %all-to-all-start.3 = ((bf16[32,2,256]{2,1,0:T(2,128)(2,1)}), bf16[32,2,256]{2,1,0:T(2,128)(2,1)S(1)}, u32[]{:S(2)}, u32[]{:S(2)}) async-start(bf16[32,2,256]{2,1,0:T(2,128)(2,1)} %reshape.256), calls=%async_computation.3 | async-start | bytes 65536 | tf_op jit(solution)/shard_map/all_to_all | solution.py:59
  84.8 1.8 %gather_fusion.1 = bf16[64,64,128]{2,1,0:T(8,128)(2,1)S(1)} fusion(bf16[32,64,128]{2,1,0:T(8,128)(2,1)} %param.21, s32[1024]{0:T(1024)S(1)} %pad_clamp_fusion), kind=kCustom, calls=%fused_computation.1 | custom fusion | bytes 2097408 | tf_op jit(solution)/shard_map/gather | solution.py:165
  86.6 3.9 %all-to-all-done.3 = bf16[32,2,256]{2,1,0:T(2,128)(2,1)S(1)} async-done(((bf16[32,2,256]{2,1,0:T(2,128)(2,1)}), bf16[32,2,256]{2,1,0:T(2,128)(2,1)S(1)}, u32[]{:S(2)}, u32[]{:S(2)}) %all-to-all-start.3) | async-done | bytes 32800 | tf_op jit(solution)/shard_map/all_to_all | solution.py:59
  90.6 1.0 convolution_convert_fusion.3
  91.7 3.4 %all-to-all-start.4 = ((bf16[8,8,4,128]{3,2,1,0:T(4,128)(2,1)}), bf16[8,8,4,128]{3,2,1,0:T(4,128)(2,1)S(1)}, u32[]{:S(2)}, u32[]{:S(2)}) async-start(bf16[8,8,4,128]{3,2,1,0:T(4,128)(2,1)} %convolution_convert_fusion.3), calls=%async_computation.4 | async-start | bytes 131072 | tf_op jit(solution)/shard_map/all_to_all | solution.py:59
  95.0 1.3 convolution_convert_fusion.1
  96.4 7.0 %all-to-all-done.4 = bf16[8,8,4,128]{3,2,1,0:T(4,128)(2,1)S(1)} async-done(((bf16[8,8,4,128]{3,2,1,0:T(4,128)(2,1)}), bf16[8,8,4,128]{3,2,1,0:T(4,128)(2,1)S(1)}, u32[]{:S(2)}, u32[]{:S(2)}) %all-to-all-start.4) | async-done | bytes 65568 | tf_op jit(solution)/shard_map/all_to_all | solution.py:59
  103.5 2.9 %fusion.9 = bf16[32,4,128]{2,0,1:T(8,128)(2,1)S(1)} fusion(f32[32,4,128]{2,0,1:T(8,128)S(1)} %fusion.28, bf16[32,4,8192]{2,0,1:T(8,128)(2,1)} %reshape.213, bf16[8192,128]{1,0:T(8,128)(2,1)} %param.13), kind=kOutput, calls=%fused_computation.20 | convolution fusion | flops 268468224 | bytes 4292608 | tf_op jit(solution)/shard_map/rsd,dh->rsh/dot_general | solution.py:142
  107.4 5.6 %all-to-all-start.5 = ((bf16[32,4,1152]{2,1,0:T(4,128)(2,1)}), bf16[32,4,1152]{2,1,0:T(4,128)(2,1)S(1)}, u32[]{:S(2)}, u32[]{:S(2)}) async-start(bf16[32,4,1152]{2,1,0:T(4,128)(2,1)} %copy.77), calls=%async_computation.5 | async-start | bytes 589824 | tf_op jit(solution)/shard_map/all_to_all | solution.py:59
  113.6 6.7 %all-to-all-done.5 = bf16[32,4,1152]{2,1,0:T(4,128)(2,1)S(1)} async-done(((bf16[32,4,1152]{2,1,0:T(4,128)(2,1)}), bf16[32,4,1152]{2,1,0:T(4,128)(2,1)S(1)}, u32[]{:S(2)}, u32[]{:S(2)}) %all-to-all-start.5) | async-done | bytes 294944 | tf_op jit(solution)/shard_map/all_to_all | solution.py:59
  122.2 11.2 %all_to_all.43 = bf16[32,1,4,128]{3,2,1,0:T(4,128)(2,1)S(1)} all-to-all(bf16[32,1,4,128]{3,2,1,0:T(4,128)(2,1)S(1)} %copy.82), channel_id=1, replica_groups=mesh['group'=8,'mp'=32] {'mp'}, dimensions={0} | all-to-all | bytes 65536 | tf_op jit(solution)/shard_map/all_to_all | solution.py:59
  133.5 2.1 %convolution_convert_fusion = bf16[32,4,8192]{2,0,1:T(8,128)(2,1)} fusion(bf16[128,8192]{1,0:T(8,128)(2,1)S(1)} %copy-done, bf16[32,1,4,128]{3,2,1,0:T(4,128)(2,1)S(1)} %all_to_all.43), kind=kOutput, calls=%fused_computation.2 | convolution fusion | flops 269484032 | bytes 4227072 | tf_op jit(solution)/shard_map/rsh,hd->rsd/dot_general | solution.py:183
  135.5 4.4 %reshape.226 = bf16[16,2,4,8192]{3,1,0,2:T(2,128)(2,1)} reshape(bf16[32,4,8192]{2,0,1:T(8,128)(2,1)} %convolution_convert_fusion) | data formatting | bytes 4194304 | tf_op jit(solution)/shard_map/reshape | solution.py:76
  139.9 5.9 %fusion.49 = (bf16[16,1,4,8192]{3,1,0,2:T(2,128)(2,1)S(1)}, bf16[16,1,4,8192]{3,1,0,2:T(2,128)(2,1)S(1)}) fusion(bf16[16,2,4,8192]{3,1,0,2:T(2,128)(2,1)} %reshape.226), kind=kLoop, calls=%fused_computation.93 | loop fusion | bytes 4194304 | tf_op jit(solution)/shard_map/slice | solution.py:77
  145.8 2.2 %select_bitcast_fusion = bf16[16,4,8192]{2,0,1:T(8,128)(2,1)S(1)} fusion(pred[]{:T(512)S(6)} %eq.18, bf16[16,1,4,8192]{3,1,0,2:T(2,128)(2,1)S(1)} %get-tuple-element.6, bf16[16,1,4,8192]{3,1,0,2:T(2,128)(2,1)S(1)} %get-tuple-element.5), kind=kLoop, calls=%fused_computation.26 | loop fusion | flops 524288 | bytes 3145729 | tf_op jit(solution)/shard_map/jit(_where)/select_n | solution.py:78
  148.2 2.5 %collective-permute-done.1 = bf16[16,4,8192]{2,0,1:T(8,128)(2,1)S(1)} collective-permute-done((bf16[16,4,8192]{2,0,1:T(8,128)(2,1)S(1)}, bf16[16,4,8192]{2,0,1:T(8,128)(2,1)S(1)}, u32[]{:S(2)}, u32[]{:S(2)}) %collective-permute-start.1) | collective-permute-done | bytes 1048608 | tf_op jit(solution)/shard_map/ppermute | solution.py:51
  150.8 3.5 %fusion = bf16[16,4,8192]{2,0,1:T(8,128)(2,1)S(1)} fusion(bf16[16,4,8192]{2,0,1:T(8,128)(2,1)S(1)} %collective-permute-done.1, pred[]{:T(512)S(6)} %eq.18, bf16[16,1,4,8192]{3,1,0,2:T(2,128)(2,1)S(1)} %get-tuple-element.6, bf16[16,1,4,8192]{3,1,0,2:T(2,128)(2,1)S(1)} %get-tuple-element.5), kind=kLoop, calls=%fused_computation.5 | loop fusion | flops 2621440 | bytes 4194305 | tf_op jit(solution)/shard_map/convert_element_type | solution.py:80
  155.1 20.0 %all_to_all.44 = bf16[16,4,8192]{2,1,0:T(4,128)(2,1)S(1)} all-to-all(bf16[16,4,8192]{2,1,0:T(4,128)(2,1)S(1)} %copy.86), channel_id=1, replica_groups={{0,2,4,6,8,10,12,14,16,18,20,22,24,26,28,30},{1,3,5,7,9,11,13,15,17,19,..., dimensions={0} | all-to-all | bytes 2097152 | tf_op jit(solution)/shard_map/all_to_all | solution.py:59
  (62 shorter events, 10.2 us)
Async XLA Ops:
  0.0 133.5 %copy-start = (bf16[128,8192]{1,0:T(8,128)(2,1)S(1)}, bf16[128,8192]{1,0:T(8,128)(2,1)}, u32[]{:S(2)}) copy-start(bf16[128,8192]{1,0:T(8,128)(2,1)} %param.15) | copy-start | bytes 6291460
  3.3 23.3 %copy-start.5 = (s32[32]{0:T(128)S(1)}, s32[32]{0:T(128)}, u32[]{:S(2)}) copy-start(s32[32]{0:T(128)} %param.19) | copy-start | bytes 388
  26.6 3.0 %collective-permute-start = (bf16[16,4,8192]{2,0,1:T(8,128)(2,1)}, bf16[16,4,8192]{2,0,1:T(8,128)(2,1)}, u32[]{:S(2)}, u32[]{:S(2)}) collective-permute-start(bf16[16,4,8192]{2,0,1:T(8,128)(2,1)} %copy.71), channel_id=1, source_target_pairs={{0,1},{1,0},{2,3},{3,2},{4,5},{5,4},{6,7},{7,6},{8,9},{9,8},{10,11... | collective-permute-start | bytes 3145736 | tf_op jit(solution)/shard_map/ppermute | solution.py:51
  35.7 25.6 %copy-start.1 = (bf16[32,64,256]{2,1,0:T(8,128)(2,1)S(1)}, bf16[32,64,256]{2,1,0:T(8,128)(2,1)}, u32[]{:S(2)}) copy-start(bf16[32,64,256]{2,1,0:T(8,128)(2,1)} %param.20) | copy-start | bytes 3145732
  79.3 11.2 %all-to-all-start.3 = ((bf16[32,2,256]{2,1,0:T(2,128)(2,1)}), bf16[32,2,256]{2,1,0:T(2,128)(2,1)S(1)}, u32[]{:S(2)}, u32[]{:S(2)}) async-start(bf16[32,2,256]{2,1,0:T(2,128)(2,1)} %reshape.256), calls=%async_computation.3 | async-start | bytes 65536 | tf_op jit(solution)/shard_map/all_to_all | solution.py:59
  91.7 11.7 %all-to-all-start.4 = ((bf16[8,8,4,128]{3,2,1,0:T(4,128)(2,1)}), bf16[8,8,4,128]{3,2,1,0:T(4,128)(2,1)S(1)}, u32[]{:S(2)}, u32[]{:S(2)}) async-start(bf16[8,8,4,128]{3,2,1,0:T(4,128)(2,1)} %convolution_convert_fusion.3), calls=%async_computation.4 | async-start | bytes 131072 | tf_op jit(solution)/shard_map/all_to_all | solution.py:59
  106.5 14.3 %copy-start.2 = (bf16[1,4,1024,128]{3,2,1,0:T(8,128)(2,1)S(1)}, bf16[1,4,1024,128]{3,2,1,0:T(8,128)(2,1)}, u32[]{:S(2)}) copy-start(bf16[1,4,1024,128]{3,2,1,0:T(8,128)(2,1)} %param.16) | copy-start | bytes 3145732
  107.4 13.0 %all-to-all-start.5 = ((bf16[32,4,1152]{2,1,0:T(4,128)(2,1)}), bf16[32,4,1152]{2,1,0:T(4,128)(2,1)S(1)}, u32[]{:S(2)}, u32[]{:S(2)}) async-start(bf16[32,4,1152]{2,1,0:T(4,128)(2,1)} %copy.77), calls=%async_computation.5 | async-start | bytes 589824 | tf_op jit(solution)/shard_map/all_to_all | solution.py:59
  120.3 1.3 copy-start.4
  148.0 2.7 %collective-permute-start.1 = (bf16[16,4,8192]{2,0,1:T(8,128)(2,1)S(1)}, bf16[16,4,8192]{2,0,1:T(8,128)(2,1)S(1)}, u32[]{:S(2)}, u32[]{:S(2)}) collective-permute-start(bf16[16,4,8192]{2,0,1:T(8,128)(2,1)S(1)} %select_bitcast_fusion), channel_id=1, source_target_pairs={{0,1},{1,0},{2,3},{3,2},{4,5},{5,4},{6,7},{7,6},{8,9},{9,8},{10,11... | collective-permute-start | bytes 3145736 | tf_op jit(solution)/shard_map/ppermute | solution.py:51
  155.1 20.4 %copy-start.3 = (bf16[1,4,8192]{2,1,0:T(4,128)(2,1)S(1)}, bf16[1,4,8192]{2,1,0:T(4,128)(2,1)}, u32[]{:S(2)}) copy-start(bf16[1,4,8192]{2,1,0:T(4,128)(2,1)} %param.11) | copy-start | bytes 196612
